TPU v7x, 32 devices: a whole 2x2x4 slice. The times are simulated.
32 devices in a mesh: section: 2 (over core), ctx: 8 (over z, x), tp: 2 (over y).
Axes of the slice: x: 2, y: 2, z: 4, core: 2. Of those that a mesh axis runs over, the one named last changes fastest.
Arguments:
- layer_input: bfloat16 [2, 1024, 1024], P(None, 'ctx'), may hold values from -6 to 6
- cotangent: bfloat16 [2, 1024, 1024], P(None, 'ctx'), may hold values from -6 to 6
- w_qkv: bfloat16 [2, 1024, 3, 1024], P('section', None, None, 'tp'), may hold values from -0.1875 to 0.1875
- b_qv: bfloat16 [2, 2, 1024], P('section', None, 'tp'), may hold values from -3 to 3
- w_out: bfloat16 [2, 1024, 1024], P('section', 'tp'), may hold values from -4 to 4
- b_out: bfloat16 [2, 1024], P('section'), may hold values from -3 to 3
- w_fc: bfloat16 [2, 1024, 4096], P('section', None, 'tp'), may hold values from -0.1875 to 0.1875
- b_fc: bfloat16 [2, 4096], P('section', 'tp'), may hold values from -3 to 3
- w_proj: bfloat16 [2, 4096, 1024], P('section', 'tp'), may hold values from -0.09375 to 0.09375
- b_proj: bfloat16 [2, 1024], P('section'), may hold values from -3 to 3
- ln_gain: float32 [2, 2, 1024], P('section'), may hold values from 0.5 to 1.5
- ln_bias: float32 [2, 2, 1024], P('section'), may hold values from -3 to 3
Outputs:
- activations: bfloat16 [2, 2, 1024, 1024], P('section', None, 'ctx')
- input_grads: float32 [2, 2, 1024, 1024], P('section', None, 'ctx')
- grad_w_qkv: float32 [2, 1024, 3, 1024], P('section', None, None, 'tp')
- grad_b_qv: float32 [2, 2, 1024], P('section', None, 'tp')
- grad_w_out: float32 [2, 1024, 1024], P('section', 'tp')
- grad_b_out: float32 [2, 1024], P('section')
- grad_w_fc: float32 [2, 1024, 4096], P('section', None, 'tp')
- grad_b_fc: float32 [2, 4096], P('section', 'tp')
- grad_w_proj: float32 [2, 4096, 1024], P('section', 'tp')
- grad_b_proj: float32 [2, 1024], P('section')
- grad_ln_gain: float32 [2, 2, 1024], P('section')
- grad_ln_bias: float32 [2, 2, 1024], P('section')
All inputs are finite; a program needn't handle non-finite values.
Results may differ from a plain program's by a relative error of at most 0.028.
Values may be sent and summed in bfloat16 or wider, within the bound.
A program may use at most 192 MiB of HBM per device.

v0:
```python
import jax
import jax.numpy as jnp
from jax import lax
from jax.sharding import PartitionSpec as P

HD = 64
EPS = 1e-05
GELU_C = 0.7978845608028654


def shifted(value, axis, steps):
    count = lax.axis_size(axis)
    first, last = (max(0, -steps), min(count, count - steps))
    return lax.ppermute(value, axis, [(source, source + steps) for source in range(first, last)])


def norm_forward(values, gain_vec, shift_vec):
    row_mean = jnp.mean(values, axis=-1, keepdims=True)
    centered = values - row_mean
    inv_std = lax.rsqrt(jnp.mean(centered * centered, axis=-1, keepdims=True) + EPS)
    normed = centered * inv_std
    return (normed * gain_vec + shift_vec, normed, inv_std)


def norm_backward(upstream, normed, inv_std, gain_vec):
    dnormed = upstream * gain_vec
    centered_grad = (
        dnormed
        - jnp.mean(dnormed, axis=-1, keepdims=True)
        - normed * jnp.mean(dnormed * normed, axis=-1, keepdims=True)
    )
    return (inv_std * centered_grad, jnp.sum(upstream * normed, axis=0), jnp.sum(upstream, axis=0))


def gelu_parts(pre_act):
    tanh_val = jnp.tanh(GELU_C * (pre_act + 0.044715 * pre_act * pre_act * pre_act))
    gelu_value = 0.5 * pre_act * (1.0 + tanh_val)
    gelu_slope = 0.5 * (1.0 + tanh_val) + 0.5 * pre_act * (1.0 - tanh_val * tanh_val) * GELU_C * (
        1.0 + 3.0 * 0.044715 * pre_act * pre_act
    )
    return (gelu_value, gelu_slope)


def split_heads(values, head_count):
    return values.reshape(values.shape[0], head_count, values.shape[1] // head_count)


def fold_keys(running, block_kv, queries, query_pos, head_count):
    totals, accum = running
    key_rows, val_rows = block_kv
    head_q = split_heads(queries, head_count)
    head_k = split_heads(key_rows, head_count)
    head_v = split_heads(val_rows, head_count)
    score_scale = HD ** (-0.5)
    scores = (
        jnp.einsum("qhd,khd->hqk", head_q, head_k, preferred_element_type=jnp.float32) * score_scale
    )
    key_pos = jnp.arange(key_rows.shape[0], dtype=jnp.int32)
    causal = query_pos[:, None] >= key_pos[None, :]
    weights = jnp.where(causal[None], jnp.exp(scores), 0.0)
    totals = jnp.sum(weights, axis=-1).T
    portion = jnp.einsum(
        "hqk,khd->qhd", weights.astype(jnp.bfloat16), head_v, preferred_element_type=jnp.float32
    )
    return (totals, portion.reshape(accum.shape))


def layer_forward(layer_in, weights_set, query_pos):
    w_qkv, b_qv, w_out, b_out, w_fc, b_fc, w_proj, b_proj, ln_gain, ln_bias = weights_set
    row_count, model_width = layer_in.shape
    local_cols = w_qkv.shape[2]
    head_count = local_cols // HD
    layer_f32 = layer_in.astype(jnp.float32)
    first_norm, normed_a, inv_a = norm_forward(layer_f32, ln_gain[0], ln_bias[0])
    first_bf = first_norm.astype(jnp.bfloat16)
    joined = jnp.dot(
        first_bf, w_qkv.reshape(model_width, 3 * local_cols), preferred_element_type=jnp.float32
    )
    queries = (joined[:, :local_cols] + b_qv[0].astype(jnp.float32)).astype(jnp.bfloat16)
    key_rows = joined[:, local_cols : 2 * local_cols].astype(jnp.bfloat16)
    val_rows = (joined[:, 2 * local_cols :] + b_qv[1].astype(jnp.float32)).astype(jnp.bfloat16)
    init_state = (
        jnp.zeros((row_count, head_count), jnp.float32),
        jnp.zeros((row_count, local_cols), jnp.float32),
    )
    totals, accum = fold_keys(
        init_state,
        (
            lax.all_gather(key_rows, "ctx", axis=0, tiled=True),
            lax.all_gather(val_rows, "ctx", axis=0, tiled=True),
        ),
        queries,
        query_pos,
        head_count,
    )
    held_keys = (key_rows, val_rows)
    attended = (
        (accum.reshape(row_count, head_count, HD) / totals[:, :, None])
        .reshape(row_count, local_cols)
        .astype(jnp.bfloat16)
    )
    log_total = jnp.log(totals)
    attn_mixed = lax.psum(
        jnp.dot(attended, w_out, preferred_element_type=jnp.float32).astype(jnp.bfloat16), "tp"
    ).astype(jnp.float32)
    hidden_in = layer_f32 + attn_mixed + b_out.astype(jnp.float32)
    second_norm, normed_b, inv_b = norm_forward(hidden_in, ln_gain[1], ln_bias[1])
    second_bf = second_norm.astype(jnp.bfloat16)
    pre_act = jnp.dot(second_bf, w_fc, preferred_element_type=jnp.float32) + b_fc.astype(
        jnp.float32
    )
    gelu_value, gelu_slope = gelu_parts(pre_act)
    act_bf = gelu_value.astype(jnp.bfloat16)
    mlp_mixed = lax.psum(
        jnp.dot(act_bf, w_proj, preferred_element_type=jnp.float32).astype(jnp.bfloat16), "tp"
    ).astype(jnp.float32)
    result = hidden_in + mlp_mixed + b_proj.astype(jnp.float32)
    saved = (
        normed_a,
        inv_a,
        first_bf,
        queries,
        (key_rows, val_rows),
        held_keys,
        attended,
        log_total,
        normed_b,
        inv_b,
        second_bf,
        act_bf,
        gelu_slope,
    )
    return (result.astype(jnp.bfloat16), saved)


def layer_backward(upstream, saved, weights_set, query_pos):
    w_qkv, b_qv, w_out, b_out, w_fc, b_fc, w_proj, b_proj, ln_gain, ln_bias = weights_set
    (
        normed_a,
        inv_a,
        first_bf,
        queries,
        own_kv,
        held_keys,
        attended,
        log_total,
        normed_b,
        inv_b,
        second_bf,
        act_bf,
        gelu_slope,
    ) = saved
    row_count, model_width = upstream.shape
    local_cols = w_qkv.shape[2]
    head_count = local_cols // HD
    score_scale = HD ** (-0.5)
    up_bf = upstream.astype(jnp.bfloat16)
    grad_b_proj = jnp.sum(upstream, axis=0)
    grad_w_proj = jnp.dot(act_bf.T, up_bf, preferred_element_type=jnp.float32)
    d_pre = jnp.dot(up_bf, w_proj.T, preferred_element_type=jnp.float32) * gelu_slope
    d_pre_bf = d_pre.astype(jnp.bfloat16)
    grad_b_fc = jnp.sum(d_pre, axis=0)
    grad_w_fc = jnp.dot(second_bf.T, d_pre_bf, preferred_element_type=jnp.float32)
    d_second = lax.psum(
        jnp.dot(d_pre_bf, w_fc.T, preferred_element_type=jnp.float32).astype(jnp.bfloat16), "tp"
    ).astype(jnp.float32)
    d_hidden_ln, gain_b, shift_b = norm_backward(d_second, normed_b, inv_b, ln_gain[1])
    d_hidden = upstream + d_hidden_ln
    grad_b_out = jnp.sum(d_hidden, axis=0)
    hidden_bf = d_hidden.astype(jnp.bfloat16)
    grad_w_out = jnp.dot(attended.T, hidden_bf, preferred_element_type=jnp.float32)
    d_attended = jnp.dot(hidden_bf, w_out.T, preferred_element_type=jnp.float32).astype(
        jnp.bfloat16
    )
    all_keys, all_vals = (
        lax.all_gather(held_keys[0], "ctx", axis=0, tiled=True),
        lax.all_gather(held_keys[1], "ctx", axis=0, tiled=True),
    )
    head_q = split_heads(queries, head_count)
    head_k = split_heads(all_keys, head_count)
    head_v = split_heads(all_vals, head_count)
    head_d = split_heads(d_attended, head_count)
    scores = (
        jnp.einsum("qhd,khd->hqk", head_q, head_k, preferred_element_type=jnp.float32) * score_scale
    )
    key_pos = jnp.arange(all_keys.shape[0], dtype=jnp.int32)
    causal = query_pos[:, None] >= key_pos[None, :]
    probs = jnp.where(causal[None], jnp.exp(scores - log_total.T[:, :, None]), 0.0)
    row_delta = jnp.sum(
        d_attended.astype(jnp.float32).reshape(row_count, head_count, HD)
        * attended.astype(jnp.float32).reshape(row_count, head_count, HD),
        axis=-1,
    )
    d_probs = jnp.einsum("qhd,khd->hqk", head_d, head_v, preferred_element_type=jnp.float32)
    d_scores = (probs * (d_probs - row_delta.T[:, :, None])).astype(jnp.bfloat16)
    d_query = (
        jnp.einsum("hqk,khd->qhd", d_scores, head_k, preferred_element_type=jnp.float32).reshape(
            row_count, local_cols
        )
        * score_scale
    )
    key_term = (
        jnp.einsum("hqk,qhd->khd", d_scores, head_q, preferred_element_type=jnp.float32).reshape(
            all_keys.shape[0], local_cols
        )
        * score_scale
    )
    val_term = jnp.einsum(
        "hqk,qhd->khd", probs.astype(jnp.bfloat16), head_d, preferred_element_type=jnp.float32
    ).reshape(all_keys.shape[0], local_cols)
    d_key, d_val = (
        lax.psum_scatter(
            key_term.astype(jnp.bfloat16), "ctx", scatter_dimension=0, tiled=True
        ).astype(jnp.float32),
        lax.psum_scatter(
            val_term.astype(jnp.bfloat16), "ctx", scatter_dimension=0, tiled=True
        ).astype(jnp.float32),
    )
    grad_b_qv = jnp.stack([jnp.sum(d_query, axis=0), jnp.sum(d_val, axis=0)])
    d_joined = jnp.concatenate([d_query, d_key, d_val], axis=1).astype(jnp.bfloat16)
    grad_w_qkv = jnp.dot(first_bf.T, d_joined, preferred_element_type=jnp.float32).reshape(
        model_width, 3, local_cols
    )
    d_first = lax.psum(
        jnp.dot(
            d_joined,
            w_qkv.reshape(model_width, 3 * local_cols).T,
            preferred_element_type=jnp.float32,
        ).astype(jnp.bfloat16),
        "tp",
    ).astype(jnp.float32)
    d_in_ln, gain_a, shift_a = norm_backward(d_first, normed_a, inv_a, ln_gain[0])
    d_input = d_hidden + d_in_ln
    grads = (
        grad_w_qkv,
        grad_b_qv,
        grad_w_out,
        grad_b_out,
        grad_w_fc,
        grad_b_fc,
        grad_w_proj,
        grad_b_proj,
        jnp.stack([gain_a, gain_b]),
        jnp.stack([shift_a, shift_b]),
    )
    return (d_input, grads)


def body(
    layer_input, cotangent, w_qkv, b_qv, w_out, b_out, w_fc, b_fc, w_proj, b_proj, ln_gain, ln_bias
):
    weights_set = (
        w_qkv[0],
        b_qv[0],
        w_out[0],
        b_out[0],
        w_fc[0],
        b_fc[0],
        w_proj[0],
        b_proj[0],
        ln_gain[0],
        ln_bias[0],
    )
    later_segment = lax.axis_index("section") == 1
    micro, row_count, model_width = layer_input.shape
    query_pos = lax.axis_index("ctx") * row_count + jnp.arange(row_count, dtype=jnp.int32)
    incoming = jnp.zeros((row_count, model_width), jnp.bfloat16)
    results = []
    saved_ticks = []
    for tick_index in range(micro + 1):
        if tick_index < micro:
            fresh_input = layer_input[tick_index]
        else:
            fresh_input = jnp.zeros((row_count, model_width), jnp.bfloat16)
        layer_in = jnp.where(later_segment, incoming, fresh_input)
        result, saved = layer_forward(layer_in, weights_set, query_pos)
        results.append(result)
        saved_ticks.append(saved)
        if tick_index < micro:
            incoming = shifted(result, "section", 1)
    outgoing = jnp.zeros((row_count, model_width), jnp.float32)
    grad_totals = []
    input_grads_all = []
    for tick_index in range(micro + 1):
        if tick_index < micro:
            given_grad = cotangent[tick_index].astype(jnp.float32)
        else:
            given_grad = jnp.zeros((row_count, model_width), jnp.float32)
        upstream = jnp.where(later_segment, given_grad, outgoing)
        saved = jax.tree.map(
            lambda late_val, early_val: jnp.where(later_segment, late_val, early_val),
            saved_ticks[min(tick_index + 1, micro)],
            saved_ticks[max(tick_index - 1, 0)],
        )
        d_input, grads = layer_backward(upstream, saved, weights_set, query_pos)
        if tick_index == 0:
            grad_totals = grads
        else:
            grad_totals = jax.tree.map(jnp.add, grad_totals, grads)
        input_grads_all.append(d_input)
        if tick_index < micro:
            outgoing = shifted(d_input.astype(jnp.bfloat16), "section", -1).astype(d_input.dtype)
    activations = jnp.stack(
        [
            jnp.where(later_segment, results[batch_index + 1], results[batch_index])
            for batch_index in range(micro)
        ]
    )[None]
    input_grads = jnp.stack(
        [
            jnp.where(later_segment, input_grads_all[batch_index], input_grads_all[batch_index + 1])
            for batch_index in range(micro)
        ]
    )[None]
    summed = (
        lax.psum(grad_totals[0].astype(jnp.bfloat16), "ctx").astype(jnp.float32),
        lax.psum(grad_totals[1].astype(jnp.bfloat16), "ctx").astype(jnp.float32),
        lax.psum(grad_totals[2].astype(jnp.bfloat16), "ctx").astype(jnp.float32),
        lax.psum(grad_totals[3].astype(jnp.bfloat16), "ctx").astype(jnp.float32),
        lax.psum(grad_totals[4].astype(jnp.bfloat16), "ctx").astype(jnp.float32),
        lax.psum(grad_totals[5].astype(jnp.bfloat16), "ctx").astype(jnp.float32),
        lax.psum(grad_totals[6].astype(jnp.bfloat16), "ctx").astype(jnp.float32),
        lax.psum(grad_totals[7].astype(jnp.bfloat16), "ctx").astype(jnp.float32),
        lax.psum(grad_totals[8].astype(jnp.bfloat16), "ctx").astype(jnp.float32),
        lax.psum(grad_totals[9].astype(jnp.bfloat16), "ctx").astype(jnp.float32),
    )
    return (
        activations,
        input_grads,
        summed[0][None],
        summed[1][None],
        summed[2][None],
        summed[3][None],
        summed[4][None],
        summed[5][None],
        summed[6][None],
        summed[7][None],
        summed[8][None],
        summed[9][None],
    )


def solution(mesh):
    placed = (
        P(None, "ctx", None),
        P(None, "ctx", None),
        P("section", None, None, "tp"),
        P("section", None, "tp"),
        P("section", "tp", None),
        P("section", None),
        P("section", None, "tp"),
        P("section", "tp"),
        P("section", "tp", None),
        P("section", None),
        P("section", None, None),
        P("section", None, None),
    )
    return jax.shard_map(
        body,
        mesh=mesh,
        in_specs=placed,
        out_specs=(
            P("section", None, "ctx", None),
            P("section", None, "ctx", None),
            P("section", None, None, "tp"),
            P("section", None, "tp"),
            P("section", "tp", None),
            P("section", None),
            P("section", None, "tp"),
            P("section", "tp"),
            P("section", "tp", None),
            P("section", None),
            P("section", None, None),
            P("section", None, None),
        ),
        check_vma=False,
    )
```

profile of v0, /device:TPU:0, one launch (start us, length us, event | category | flops | bytes accessed | tf_op | source)
XLA Modules:
  0.0 1655.5 jit_solution(18073447266085569030)
XLA Ops:
  11.3 4.7 copy.76
  21.0 42.0 %all-gather.15.cloned.1.call-done = bf16[1024,512]{1,0:T(8,128)(2,1)} async-done(((bf16[128,512]{1,0:T(8,128)(2,1)}), bf16[1024,512]{1,0:T(8,128)(2,1)}) %all-gather.15.cloned.1.call-update) | async-done | bytes 1048592 | tf_op jit(solution)/shard_map/all_gather | solution.py:89
  65.2 4.4 fusion.24
  69.6 34.5 %all-gather.13.cloned.1.call-done = bf16[1024,512]{1,0:T(8,128)(2,1)} async-done(((bf16[128,512]{1,0:T(8,128)(2,1)}), bf16[1024,512]{1,0:T(8,128)(2,1)}) %all-gather.13.cloned.1.call-update) | async-done | bytes 1048592 | tf_op jit(solution)/shard_map/all_gather | solution.py:90
  105.6 3.1 fusion.138
  109.9 22.1 %all-reduce.16.cloned.1.call-done = bf16[128,1024]{1,0:T(8,128)(2,1)} async-done(((bf16[128,1024]{1,0:T(8,128)(2,1)}), bf16[128,1024]{1,0:T(8,128)(2,1)}) %all-reduce.16.cloned.1.call-update) | async-done | bytes 262160 | tf_op jit(solution)/shard_map/psum | solution.py:103
  134.5 3.1 fusion.35
  139.4 23.4 %all-reduce.18.cloned.1.call-done = bf16[128,1024]{1,0:T(8,128)(2,1)} async-done(((bf16[128,1024]{1,0:T(8,128)(2,1)}), bf16[128,1024]{1,0:T(8,128)(2,1)}) %all-reduce.18.cloned.1.call-update) | async-done | bytes 262160 | tf_op jit(solution)/shard_map/psum | solution.py:114
  173.6 39.7 %all-gather.19.cloned.1.call-done = bf16[1024,512]{1,0:T(8,128)(2,1)} async-done(((bf16[128,512]{1,0:T(8,128)(2,1)}), bf16[1024,512]{1,0:T(8,128)(2,1)}) %all-gather.19.cloned.1.call-update) | async-done | bytes 1048592 | tf_op jit(solution)/shard_map/all_gather | solution.py:89
  215.6 5.0 fusion.26
  220.6 33.7 %all-gather.17.cloned.1.call-done = bf16[1024,512]{1,0:T(8,128)(2,1)} async-done(((bf16[128,512]{1,0:T(8,128)(2,1)}), bf16[1024,512]{1,0:T(8,128)(2,1)}) %all-gather.17.cloned.1.call-update) | async-done | bytes 1048592 | tf_op jit(solution)/shard_map/all_gather | solution.py:90
  256.6 3.4 fusion.132
  261.6 21.6 %all-reduce.20.cloned.1.call-done = bf16[128,1024]{1,0:T(8,128)(2,1)} async-done(((bf16[128,1024]{1,0:T(8,128)(2,1)}), bf16[128,1024]{1,0:T(8,128)(2,1)}) %all-reduce.20.cloned.1.call-update) | async-done | bytes 262160 | tf_op jit(solution)/shard_map/psum | solution.py:103
  286.2 3.1 fusion.38
  297.9 28.0 %all-reduce.34.cloned.1.call-done = (bf16[128,1024]{1,0:T(8,128)(2,1)}, bf16[128,1024]{1,0:T(8,128)(2,1)}) async-done(((bf16[128,1024]{1,0:T(8,128)(2,1)}, bf16[128,1024]{1,0:T(8,128)(2,1)}), (bf16[128,1024]{1,0:T(8,128)(2,1)}, bf16[128,1024]{1,0:T(8,128)(2,1)})) %all-reduce.34.cloned.1.call-update) | async-done | bytes 524304 | tf_op jit(solution)/shard_map/psum | solution.py:164
  338.4 30.5 %all-gather.25.cloned.1.call-done = bf16[1024,512]{1,0:T(8,128)(2,1)} async-done(((bf16[128,512]{1,0:T(8,128)(2,1)}), bf16[1024,512]{1,0:T(8,128)(2,1)}) %all-gather.25.cloned.1.call-update) | async-done | bytes 1048592 | tf_op jit(solution)/shard_map/all_gather | solution.py:176
  371.2 4.0 fusion.384
  381.8 28.1 %all-gather.23.cloned.1.call-done = bf16[1024,512]{1,0:T(8,128)(2,1)} async-done(((bf16[128,512]{1,0:T(8,128)(2,1)}), bf16[1024,512]{1,0:T(8,128)(2,1)}) %all-gather.23.cloned.1.call-update) | async-done | bytes 1048592 | tf_op jit(solution)/shard_map/all_gather | solution.py:89
  412.2 4.6 fusion.28
  422.1 28.9 %all-gather.27.cloned.1.call-done = bf16[1024,512]{1,0:T(8,128)(2,1)} async-done(((bf16[128,512]{1,0:T(8,128)(2,1)}), bf16[1024,512]{1,0:T(8,128)(2,1)}) %all-gather.27.cloned.1.call-update) | async-done | bytes 1048592 | tf_op jit(solution)/shard_map/all_gather | solution.py:177
  454.9 4.2 multiply_convert_fusion.2
  464.2 27.8 %all-gather.21.cloned.1.call-done = bf16[1024,512]{1,0:T(8,128)(2,1)} async-done(((bf16[128,512]{1,0:T(8,128)(2,1)}), bf16[1024,512]{1,0:T(8,128)(2,1)}) %all-gather.21.cloned.1.call-update) | async-done | bytes 1048592 | tf_op jit(solution)/shard_map/all_gather | solution.py:90
  494.3 3.5 fusion.126
  500.4 58.6 %reduce-scatter.21.cloned.1.call-done = bf16[128,512]{1,0:T(8,128)(2,1)} async-done(((bf16[1024,512]{1,0:T(8,128)(2,1)}), bf16[128,512]{1,0:T(8,128)(2,1)}) %reduce-scatter.21.cloned.1.call-update) | async-done | bytes 131088
  560.1 65.4 %reduce-scatter.19.cloned.1.call-done = bf16[128,512]{1,0:T(8,128)(2,1)} async-done(((bf16[1024,512]{1,0:T(8,128)(2,1)}), bf16[128,512]{1,0:T(8,128)(2,1)}) %reduce-scatter.19.cloned.1.call-update) | async-done | bytes 131088
  626.5 3.3 convolution_convert_fusion.2
  631.6 26.0 %all-reduce.32.cloned.1.call-done = (bf16[128,1024]{1,0:T(8,128)(2,1)}, bf16[128,1024]{1,0:T(8,128)(2,1)}) async-done(((bf16[128,1024]{1,0:T(8,128)(2,1)}, bf16[128,1024]{1,0:T(8,128)(2,1)}), (bf16[128,1024]{1,0:T(8,128)(2,1)}, bf16[128,1024]{1,0:T(8,128)(2,1)})) %all-reduce.32.cloned.1.call-update) | async-done | bytes 524304 | tf_op jit(solution)/shard_map/psum | solution.py:224
  666.7 3.2 fusion.41
  670.0 3.1 fusion.383
  677.7 22.7 %all-gather.29.cloned.1.call-done = bf16[1024,512]{1,0:T(8,128)(2,1)} async-done(((bf16[128,512]{1,0:T(8,128)(2,1)}), bf16[1024,512]{1,0:T(8,128)(2,1)}) %all-gather.29.cloned.1.call-update) | async-done | bytes 1048592 | tf_op jit(solution)/shard_map/all_gather | solution.py:176
  702.7 4.0 fusion.385
  706.7 18.5 %all-reduce.22.cloned.1.call-done = bf16[128,1024]{1,0:T(8,128)(2,1)} async-done(((bf16[128,1024]{1,0:T(8,128)(2,1)}), bf16[128,1024]{1,0:T(8,128)(2,1)}) %all-reduce.22.cloned.1.call-update) | async-done | bytes 262160 | tf_op jit(solution)/shard_map/psum | solution.py:164
  732.0 4.3 fusion.89
  738.7 28.7 %all-gather.31.cloned.1.call-done = bf16[1024,512]{1,0:T(8,128)(2,1)} async-done(((bf16[128,512]{1,0:T(8,128)(2,1)}), bf16[1024,512]{1,0:T(8,128)(2,1)}) %all-gather.31.cloned.1.call-update) | async-done | bytes 1048592 | tf_op jit(solution)/shard_map/all_gather | solution.py:177
  771.4 4.2 multiply_convert_fusion.1
  780.7 6.1 fusion.275
  786.9 4.9 fusion.245
  795.2 13.4 all-gather.33.cloned.1.call-done
  810.9 38.7 %all-gather.35.cloned.1.call-done = bf16[1024,512]{1,0:T(8,128)(2,1)} async-done(((bf16[128,512]{1,0:T(8,128)(2,1)}), bf16[1024,512]{1,0:T(8,128)(2,1)}) %all-gather.35.cloned.1.call-update) | async-done | bytes 1048592 | tf_op jit(solution)/shard_map/all_gather | solution.py:177
  851.9 4.3 fusion.386
  858.3 57.7 %reduce-scatter.25.cloned.1.call-done = bf16[128,512]{1,0:T(8,128)(2,1)} async-done(((bf16[1024,512]{1,0:T(8,128)(2,1)}), bf16[128,512]{1,0:T(8,128)(2,1)}) %reduce-scatter.25.cloned.1.call-update) | async-done | bytes 131088
  917.6 65.0 %reduce-scatter.23.cloned.1.call-done = bf16[128,512]{1,0:T(8,128)(2,1)} async-done(((bf16[1024,512]{1,0:T(8,128)(2,1)}), bf16[128,512]{1,0:T(8,128)(2,1)}) %reduce-scatter.23.cloned.1.call-update) | async-done | bytes 131088
  984.3 3.4 convolution_convert_fusion.1
  988.2 4.9 fusion.280
  993.1 17.1 %all-reduce.24.cloned.1.call-done = bf16[128,1024]{1,0:T(8,128)(2,1)} async-done(((bf16[128,1024]{1,0:T(8,128)(2,1)}), bf16[128,1024]{1,0:T(8,128)(2,1)}) %all-reduce.24.cloned.1.call-update) | async-done | bytes 262160 | tf_op jit(solution)/shard_map/psum | solution.py:224
  1016.8 3.8 fusion.111
  1026.8 6.6 fusion.243
  1033.3 17.6 %all-reduce.26.cloned.1.call-done = bf16[128,1024]{1,0:T(8,128)(2,1)} async-done(((bf16[128,1024]{1,0:T(8,128)(2,1)}), bf16[128,1024]{1,0:T(8,128)(2,1)}) %all-reduce.26.cloned.1.call-update) | async-done | bytes 262160 | tf_op jit(solution)/shard_map/psum | solution.py:164
  1058.5 4.3 fusion.92
  1065.4 6.1 fusion.273
  1073.3 3.9 fusion.278
  1084.5 9.6 fusion.30
  1094.1 9.2 fusion.31
  1107.2 22.2 %reduce-scatter.29.cloned.1.call-done = bf16[128,512]{1,0:T(8,128)(2,1)} async-done(((bf16[1024,512]{1,0:T(8,128)(2,1)}), bf16[128,512]{1,0:T(8,128)(2,1)}) %reduce-scatter.29.cloned.1.call-update) | async-done | bytes 131088
  1130.5 65.4 %reduce-scatter.27.cloned.1.call-done = bf16[128,512]{1,0:T(8,128)(2,1)} async-done(((bf16[1024,512]{1,0:T(8,128)(2,1)}), bf16[128,512]{1,0:T(8,128)(2,1)}) %reduce-scatter.27.cloned.1.call-update) | async-done | bytes 131088
  1196.9 3.2 convolution_convert_fusion
  1200.3 7.5 add_convert_fusion.2
  1207.8 4.6 copy.98
  1222.7 5.3 all-reduce.30.cloned.1.call-done
  1230.8 39.5 %all-reduce = (bf16[1,2,512]{2,1,0:T(2,128)(2,1)S(1)}, bf16[1,1024]{1,0:T(2,128)(2,1)S(1)}, bf16[1,2048]{1,0:T(2,128)(2,1)S(1)}, bf16[1,1024]{1,0:T(2,128)(2,1)S...) all-reduce(bf16[1,2,512]{2,1,0:T(2,128)(2,1)S(1)} %fusion.327, ...), channel_id=1, replica_groups=mesh['section'=2,'ctx'=8,'tp'=2] {'ctx'}, use_global_device_ids=true, to_apply=%region_55.56 | all-reduce | flops 9216 | bytes 36864 | tf_op jit(solution)/shard_map/psum | solution.py:317
  1279.3 349.7 %all-reduce.28.cloned.1.call-done = (bf16[1,1024,3,512]{1,3,2,0:T(8,128)(2,1)}, bf16[1,512,1024]{2,1,0:T(8,128)(2,1)}, bf16[1,1024,2048]{2,1,0:T(8,128)(2,1)}, bf16[1,2048,1024]{2,1,0:T(8,128)(2,1)}) async-done(((bf16[1,1024,3,512]{1,3,2,0:T(8,128)(2,1)}, bf16[1,512,1024]{2,1,0:T(8,128)(2,1)}, bf16[1,1024,2048]{2,1,0:T(8,128)(2,1)}, bf16[1,2048,1024]{2,1,0:T(8,128)(2,1)}), ...) | async-done | bytes 12582928 | tf_op jit(solution)/shard_map/psum | solution.py:316
  1631.8 5.4 copy.99
  1637.2 6.8 broadcast_in_dim.177
  1644.0 4.4 broadcast_in_dim.181
  (525 shorter events, 202.8 us)
Async XLA Ops:
  7.2 101.5 %copy-start = (bf16[1,512,1024]{2,1,0:T(8,128)(2,1)S(1)}, bf16[1,512,1024]{2,1,0:T(8,128)(2,1)}, u32[]{:S(2)}) copy-start(bf16[1,512,1024]{2,1,0:T(8,128)(2,1)} %param.16) | copy-start | bytes 3145732
  7.2 55.7 %all-gather.15.cloned.1.call-start = ((), (), s32[]{:S(2)}) async-start(), calls=%async_computation.7 | async-start | bytes 1179648 | tf_op jit(solution)/shard_map/all_gather | solution.py:89
  11.2 123.3 %copy-start.80 = (f32[1,1,1024]{2,1,0:T(1,128)}, f32[1,1,1024]{2,1,0:T(1,128)S(1)}, u32[]{:S(2)}) copy-start(f32[1,1,1024]{2,1,0:T(1,128)S(1)} %get-tuple-element.132) | copy-start | bytes 12292
  19.1 50.6 %copy-start.38 = (f32[128,1536]{1,0:T(8,128)}, f32[128,1536]{1,0:T(8,128)S(1)}, u32[]{:S(2)}) copy-start(f32[128,1536]{1,0:T(8,128)S(1)} %fusion.264) | copy-start | bytes 2359300
  19.8 84.3 %all-gather.13.cloned.1.call-start = ((), (), s32[]{:S(2)}) async-start(), calls=%async_computation.6 | async-start | bytes 1179648 | tf_op jit(solution)/shard_map/all_gather | solution.py:90
  19.9 49.7 %copy-start.114 = (f32[1,1,512]{2,1,0:T(1,128)}, f32[1,1,512]{2,1,0:T(1,128)S(1)}, u32[]{:S(2)}) copy-start(f32[1,1,512]{2,1,0:T(1,128)S(1)} %get-tuple-element.136) | copy-start | bytes 6148
  19.9 49.7 %copy-start.115 = (f32[1,1,512]{2,1,0:T(1,128)}, f32[1,1,512]{2,1,0:T(1,128)S(1)}, u32[]{:S(2)}) copy-start(f32[1,1,512]{2,1,0:T(1,128)S(1)} %get-tuple-element.137) | copy-start | bytes 6148
  20.6 150.3 %copy-start.50 = (bf16[128,512]{1,0:T(8,128)(2,1)}, bf16[128,512]{1,0:T(8,128)(2,1)S(1)}, u32[]{:S(2)}) copy-start(bf16[128,512]{1,0:T(8,128)(2,1)S(1)} %get-tuple-element.120) | copy-start | bytes 393220
  20.6 111.3 %all-reduce.16.cloned.1.call-start = ((), (), s32[]{:S(2)}) async-start(), calls=%async_computation.8 | async-start | bytes 524288 | tf_op jit(solution)/shard_map/psum | solution.py:103
  21.0 84.6 %copy-start.89 = (pred[128,1024]{1,0:T(8,128)(4,1)}, pred[128,1024]{1,0:T(8,128)(4,1)S(1)}, u32[]{:S(2)}) copy-start(pred[128,1024]{1,0:T(8,128)(4,1)S(1)} %iota_compare_fusion) | copy-start | bytes 393220
  69.6 39.1 %copy-start.137 = (f32[8,128]{1,0:T(8,128)}, f32[8,128]{1,0:T(8,128)S(1)}, u32[]{:S(2)}) copy-start(f32[8,128]{1,0:T(8,128)S(1)} %get-tuple-element.147) | copy-start | bytes 12292
  109.8 53.0 %all-reduce.18.cloned.1.call-start = ((), (), s32[]{:S(2)}) async-start(), calls=%async_computation.9 | async-start | bytes 524288 | tf_op jit(solution)/shard_map/psum | solution.py:114
  137.7 153.3 %copy-start.8 = (f32[128,2048]{1,0:T(8,128)}, f32[128,2048]{1,0:T(8,128)S(1)}, u32[]{:S(2)}) copy-start(f32[128,2048]{1,0:T(8,128)S(1)} %fusion.35) | copy-start | bytes 3145732
  139.4 73.9 %all-gather.19.cloned.1.call-start = ((), (), s32[]{:S(2)}) async-start(), calls=%async_computation.11 | async-start | bytes 1179648 | tf_op jit(solution)/shard_map/all_gather | solution.py:89
  163.9 2.4 collective-permute-start
  172.8 47.7 %copy-start.67 = (bf16[128,512]{1,0:T(8,128)(2,1)}, bf16[128,512]{1,0:T(8,128)(2,1)S(1)}, u32[]{:S(2)}) copy-start(bf16[128,512]{1,0:T(8,128)(2,1)S(1)} %get-tuple-element.119) | copy-start | bytes 393220
  172.8 81.4 %all-gather.17.cloned.1.call-start = ((), (), s32[]{:S(2)}) async-start(), calls=%async_computation.10 | async-start | bytes 1179648 | tf_op jit(solution)/shard_map/all_gather | solution.py:90
  173.4 109.8 %all-reduce.20.cloned.1.call-start = ((), (), s32[]{:S(2)}) async-start(), calls=%async_computation.12 | async-start | bytes 524288 | tf_op jit(solution)/shard_map/psum | solution.py:103
  260.0 193.3 %copy-start.58 = (bf16[128,8,64]{0,2,1:T(8,128)(2,1)}, bf16[128,8,64]{0,2,1:T(8,128)(2,1)S(1)}, u32[]{:S(2)}) copy-start(bf16[128,8,64]{0,2,1:T(8,128)(2,1)S(1)} %fusion.132) | copy-start | bytes 393220
  261.0 64.9 %all-reduce.34.cloned.1.call-start = ((), (), s32[]{:S(2)}) async-start(), calls=%async_computation.33 | async-start | bytes 1048576 | tf_op jit(solution)/shard_map/psum | solution.py:164
  297.1 37.9 %copy-start.68 = (bf16[128,512]{1,0:T(8,128)(2,1)S(1)}, bf16[128,512]{1,0:T(8,128)(2,1)}, u32[]{:S(2)}) copy-start(bf16[128,512]{1,0:T(8,128)(2,1)} %copy-done.67) | copy-start | bytes 393220
  297.1 71.8 %all-gather.25.cloned.1.call-start = ((), (), s32[]{:S(2)}) async-start(), calls=%async_computation.15 | async-start | bytes 1179648 | tf_op jit(solution)/shard_map/all_gather | solution.py:176
  297.8 112.1 %all-gather.23.cloned.1.call-start = ((), (), s32[]{:S(2)}) async-start(), calls=%async_computation.14 | async-start | bytes 1179648 | tf_op jit(solution)/shard_map/all_gather | solution.py:89
  327.8 43.4 %copy-start.76 = (bf16[128,1024]{1,0:T(8,128)(2,1)}, bf16[128,1024]{1,0:T(8,128)(2,1)S(1)}, u32[]{:S(2)}) copy-start(bf16[128,1024]{1,0:T(8,128)(2,1)S(1)} %get-tuple-element.85) | copy-start | bytes 786436
  327.8 2.7 collective-permute-start.1
  336.6 44.4 %copy-start.64 = (bf16[128,512]{1,0:T(8,128)(2,1)}, bf16[128,512]{1,0:T(8,128)(2,1)S(1)}, u32[]{:S(2)}) copy-start(bf16[128,512]{1,0:T(8,128)(2,1)S(1)} %get-tuple-element.113) | copy-start | bytes 393220
  336.6 38.7 %copy-start.77 = (bf16[128,1024]{1,0:T(8,128)(2,1)S(1)}, bf16[128,1024]{1,0:T(8,128)(2,1)}, u32[]{:S(2)}) copy-start(bf16[128,1024]{1,0:T(8,128)(2,1)} %get-tuple-element.74) | copy-start | bytes 786436
  336.6 114.4 %all-gather.27.cloned.1.call-start = ((), (), s32[]{:S(2)}) async-start(), calls=%async_computation.16 | async-start | bytes 1179648 | tf_op jit(solution)/shard_map/all_gather | solution.py:177
  337.4 154.7 %all-gather.21.cloned.1.call-start = ((), (), s32[]{:S(2)}) async-start(), calls=%async_computation.13 | async-start | bytes 1179648 | tf_op jit(solution)/shard_map/all_gather | solution.py:90
  375.2 183.8 %reduce-scatter.21.cloned.1.call-start = ((), (), s32[]{:S(2)}) async-start(), calls=%async_computation.25 | async-start | bytes 1179648
  378.2 281.4 %copy-start.29 = (f32[128,1024]{1,0:T(8,128)}, f32[128,1024]{1,0:T(8,128)S(1)}, u32[]{:S(2)}) copy-start(f32[128,1024]{1,0:T(8,128)S(1)} %get-tuple-element.79) | copy-start | bytes 1572868
  421.9 203.6 %reduce-scatter.19.cloned.1.call-start = ((), (), s32[]{:S(2)}) async-start(), calls=%async_computation.24 | async-start | bytes 1179648
  464.2 193.4 %all-reduce.32.cloned.1.call-start = ((), (), s32[]{:S(2)}) async-start(), calls=%async_computation.32 | async-start | bytes 1048576 | tf_op jit(solution)/shard_map/psum | solution.py:224
  500.4 162.6 %copy-start.54 = (bf16[8,64,128]{2,1,0:T(8,128)(2,1)}, bf16[8,64,128]{2,1,0:T(8,128)(2,1)S(1)}, u32[]{:S(2)}) copy-start(bf16[8,64,128]{2,1,0:T(8,128)(2,1)S(1)} %get-tuple-element.124) | copy-start | bytes 393220
  626.5 39.0 %copy-start.56 = (bf16[128,512]{0,1:T(8,128)(2,1)}, bf16[128,512]{0,1:T(8,128)(2,1)S(1)}, u32[]{:S(2)}) copy-start(bf16[128,512]{0,1:T(8,128)(2,1)S(1)} %copy.101) | copy-start | bytes 393220
  629.8 70.6 %all-gather.29.cloned.1.call-start = ((), (), s32[]{:S(2)}) async-start(), calls=%async_computation.18 | async-start | bytes 1179648 | tf_op jit(solution)/shard_map/all_gather | solution.py:176
  631.5 93.6 %all-reduce.22.cloned.1.call-start = ((), (), s32[]{:S(2)}) async-start(), calls=%async_computation.17 | async-start | bytes 524288 | tf_op jit(solution)/shard_map/psum | solution.py:164
  663.0 6.9 collective-permute-start.2
  675.4 92.1 %all-gather.31.cloned.1.call-start = ((), (), s32[]{:S(2)}) async-start(), calls=%async_computation.19 | async-start | bytes 1179648 | tf_op jit(solution)/shard_map/all_gather | solution.py:177
  676.1 132.5 %all-gather.33.cloned.1.call-start = ((), (), s32[]{:S(2)}) async-start(), calls=%async_computation.22 | async-start | bytes 1179648 | tf_op jit(solution)/shard_map/all_gather | solution.py:176
  676.2 49.0 %copy-start.7 = (bf16[128,1024]{1,0:T(8,128)(2,1)S(1)}, bf16[128,1024]{1,0:T(8,128)(2,1)}, u32[]{:S(2)}) copy-start(bf16[128,1024]{1,0:T(8,128)(2,1)} %get-tuple-element.73) | copy-start | bytes 786436
  676.2 49.0 %copy-start.113 = (f32[128]{0:T(128)S(1)}, f32[128]{0:T(128)}, u32[]{:S(2)}) copy-start(f32[128]{0:T(128)} %copy-done.111) | copy-start | bytes 1540
  676.2 49.0 %copy-start.118 = (f32[128]{0:T(128)S(1)}, f32[128]{0:T(128)}, u32[]{:S(2)}) copy-start(f32[128]{0:T(128)} %copy-done.116) | copy-start | bytes 1540
  676.2 49.0 %copy-start.120 = (f32[128]{0:T(128)S(1)}, f32[128]{0:T(128)}, u32[]{:S(2)}) copy-start(f32[128]{0:T(128)} %copy-done.119) | copy-start | bytes 1540
  676.2 49.0 %copy-start.126 = (f32[128]{0:T(128)S(1)}, f32[128]{0:T(128)}, u32[]{:S(2)}) copy-start(f32[128]{0:T(128)} %copy-done.125) | copy-start | bytes 1540
  676.9 172.7 %all-gather.35.cloned.1.call-start = ((), (), s32[]{:S(2)}) async-start(), calls=%async_computation.23 | async-start | bytes 1179648 | tf_op jit(solution)/shard_map/all_gather | solution.py:177
  677.1 50.2 %copy-start.70 = (bf16[128,512]{0,1:T(8,128)(2,1)}, bf16[128,512]{0,1:T(8,128)(2,1)S(1)}, u32[]{:S(2)}) copy-start(bf16[128,512]{0,1:T(8,128)(2,1)S(1)} %copy.91) | copy-start | bytes 393220
  677.5 238.5 %reduce-scatter.25.cloned.1.call-start = ((), (), s32[]{:S(2)}) async-start(), calls=%async_computation.27 | async-start | bytes 1179648
  738.7 243.9 %reduce-scatter.23.cloned.1.call-start = ((), (), s32[]{:S(2)}) async-start(), calls=%async_computation.26 | async-start | bytes 1179648
  780.6 229.5 %all-reduce.24.cloned.1.call-start = ((), (), s32[]{:S(2)}) async-start(), calls=%async_computation.20 | async-start | bytes 524288 | tf_op jit(solution)/shard_map/psum | solution.py:224
  987.7 63.3 %all-reduce.26.cloned.1.call-start = ((), (), s32[]{:S(2)}) async-start(), calls=%async_computation.21 | async-start | bytes 524288 | tf_op jit(solution)/shard_map/psum | solution.py:164
  1015.3 5.3 collective-permute-start.3
  1026.7 102.7 %reduce-scatter.29.cloned.1.call-start = ((), (), s32[]{:S(2)}) async-start(), calls=%async_computation.29 | async-start | bytes 1179648
  1065.1 130.8 %reduce-scatter.27.cloned.1.call-start = ((), (), s32[]{:S(2)}) async-start(), calls=%async_computation.28 | async-start | bytes 1179648
  1084.3 143.6 %all-reduce.30.cloned.1.call-start = ((), (), s32[]{:S(2)}) async-start(), calls=%async_computation.31 | async-start | bytes 1048576 | tf_op jit(solution)/shard_map/psum | solution.py:114
  1105.7 94.6 %copy-start.99 = (f32[128]{0:T(128)S(1)}, f32[128]{0:T(128)}, u32[]{:S(2)}) copy-start(f32[128]{0:T(128)} %copy-done.98) | copy-start | bytes 1540
  1105.7 94.6 %copy-start.103 = (f32[128]{0:T(128)S(1)}, f32[128]{0:T(128)}, u32[]{:S(2)}) copy-start(f32[128]{0:T(128)} %copy-done.101) | copy-start | bytes 1540
  1105.7 94.6 %copy-start.106 = (f32[128]{0:T(128)S(1)}, f32[128]{0:T(128)}, u32[]{:S(2)}) copy-start(f32[128]{0:T(128)} %copy-done.104) | copy-start | bytes 1540
  1105.7 94.6 %copy-start.110 = (f32[128]{0:T(128)S(1)}, f32[128]{0:T(128)}, u32[]{:S(2)}) copy-start(f32[128]{0:T(128)} %copy-done.109) | copy-start | bytes 1540
  1130.5 77.3 %copy-start.48 = (bf16[128,512]{0,1:T(8,128)(2,1)}, bf16[128,512]{0,1:T(8,128)(2,1)S(1)}, u32[]{:S(2)}) copy-start(bf16[128,512]{0,1:T(8,128)(2,1)S(1)} %copy.111) | copy-start | bytes 393220
  1200.2 428.9 %all-reduce.28.cloned.1.call-start = ((), (), s32[]{:S(2)}) async-start(), calls=%async_computation.30 | async-start | bytes 25165824 | tf_op jit(solution)/shard_map/psum | solution.py:316
  1212.4 61.5 %copy-start.95 = (f32[1,1024]{1,0:T(1,128)S(1)}, f32[1,1024]{1,0:T(1,128)}, u32[]{:S(2)}) copy-start(f32[1,1024]{1,0:T(1,128)} %copy-done.93) | copy-start | bytes 12292
  1213.5 63.5 %copy-start.34 = (f32[128,1024]{1,0:T(8,128)S(1)}, f32[128,1024]{1,0:T(8,128)}, u32[]{:S(2)}) copy-start(f32[128,1024]{1,0:T(8,128)} %copy-done.33) | copy-start | bytes 1572868
  1214.1 64.1 %copy-start.49 = (f32[1,128,1024]{2,1,0:T(8,128)S(1)}, f32[1,128,1024]{2,1,0:T(8,128)}, u32[]{:S(2)}) copy-start(f32[1,128,1024]{2,1,0:T(8,128)} %get-tuple-element.82) | copy-start | bytes 1572868
  (121 other events, 1137.3 us)
Sparse Core Ops, SparseCore 0:
  19.9 42.9 all-gather.14
  65.1 38.9 all-gather.12
  109.9 21.9 all-reduce.15
  139.5 23.2 all-reduce.17
  173.0 40.2 all-gather.18
  215.3 38.9 all-gather.16
  261.2 21.9 all-reduce.19
  297.2 28.6 all-reduce.33
  328.6 40.2 all-gather.24
  370.9 38.9 all-gather.22
  412.0 38.9 all-gather.26
  453.0 38.9 all-gather.20
  496.0 62.9 reduce-scatter.20
  562.3 63.1 reduce-scatter.18
  629.9 27.6 all-reduce.31
  660.1 40.2 all-gather.28
  703.1 21.9 all-reduce.21
  727.1 40.2 all-gather.30
  769.6 38.9 all-gather.32
  810.6 38.9 all-gather.34
  853.0 62.8 reduce-scatter.24
  919.3 63.2 reduce-scatter.22
  987.8 22.3 all-reduce.23
  1026.8 24.0 all-reduce.25
  1065.2 64.1 reduce-scatter.28
  1132.7 63.1 reduce-scatter.26
  1200.3 27.6 all-reduce.29
  1233.9 395.0 all-reduce.27
where the time goes:
time: 1670 us; the launch traced here: 1660 us
  waiting for transfers between devices  1240 us (74%)
  matrix products  188 us (11%)
  local copies, waits for them, and re-layouts  87.3 us (5%)
  other arithmetic  77.7 us (5%)
  blocking collectives  39.5 us (2%)
    psum x1, waiting for transfers between devices, body(): lax.psum(grad_totals[0].astype(jnp.bfloat16), 'ctx').astype(jnp.float32)  350 us
    unnamed x34, waiting for transfers between devices  338 us
    all_gather x3, waiting for transfers between devices, layer_forward(): lax.all_gather(key_rows, 'ctx', axis=0, tiled=True)  110 us
    all_gather x3, waiting for transfers between devices, layer_backward(): lax.all_gather(held_keys[1], 'ctx', axis=0, tiled=True)  96.4 us
    all_gather x3, waiting for transfers between devices, layer_forward(): lax.all_gather(val_rows, 'ctx', axis=0, tiled=True)  96 us
    all_gather x3, waiting for transfers between devices, layer_backward(): lax.all_gather(held_keys[0], 'ctx', axis=0, tiled=True)  66.6 us
    psum x3, waiting for transfers between devices, layer_backward(): lax.psum(jnp.dot(d_pre_bf, w_fc.T, preferred_element_type=jnp.float32).as...  64.1 us
    psum x2, waiting for transfers between devices, layer_forward(): lax.psum(jnp.dot(attended, w_out, preferred_element_type=jnp.float32).ast...  43.7 us
  transfers between devices with their start and end apart: 32, of which 30 were waited for; matrix products, arithmetic and copies ran while one was open for 14% of the time, Pallas kernels for 0%

commit v1 on v0

--- a/solution.py
+++ b/solution.py
@@ -86,7 +86,9 @@
     totals, accum = fold_keys(
         init_state,
         (
-            lax.all_gather(key_rows, "ctx", axis=0, tiled=True),
+            jnp.concatenate(
+                lax.all_to_all(jnp.stack([key_rows] * lax.axis_size("ctx")), "ctx", 0, 0), axis=0
+            ),
             lax.all_gather(val_rows, "ctx", axis=0, tiled=True),
         ),
         queries,

time: 1670 us -> 1580 us (0.946)
  waiting for transfers between devices: 1240 us -> 1130 us
  starting transfers between devices: 8.31 us -> 26.7 us
    all_gather x3 -> x0, waiting for transfers between devices: 110 us -> none  [layer_forward(): lax.all_gather(key_rows, 'ctx', axis=0, tiled=True)]
    all_to_all x0 -> x3, waiting for transfers between devices: none -> 56.2 us  [layer_forward(): lax.all_to_all(jnp.stack([key_rows] * lax.axis_size('ctx')), 'ctx', 0, 0)]
    all_gather x3, waiting for transfers between devices: 96 us -> 51.3 us  [layer_forward(): lax.all_gather(val_rows, 'ctx', axis=0, tiled=True)]
    all_to_all x0 -> x3, starting transfers between devices: none -> 18.3 us  [layer_forward(): lax.all_to_all(jnp.stack([key_rows] * lax.axis_size('ctx')), 'ctx', 0, 0)]
    unnamed x320 -> x330, local copies, waits for them, and re-layouts: 42.3 us -> 43.2 us
    unnamed x34 -> x31, waiting for transfers between devices: 338 us -> 337 us
  transfers between devices with their start and end apart: 32 -> 32, of which waited for: 30 -> 29; matrix products, arithmetic and copies ran while one was open for 14% -> 15% of each run, Pallas kernels for 0% -> 0%
where the time goes in v1:
time: 1580 us; the launch traced here: 1570 us
  waiting for transfers between devices  1130 us (72%)
  matrix products  187 us (12%)
  local copies, waits for them, and re-layouts  97.5 us (6%)
  other arithmetic  78 us (5%)
  blocking collectives  38.9 us (2%)
  starting transfers between devices  26.7 us (2%)
  between operations  16.1 us (1%)
    psum x1, waiting for transfers between devices, body(): lax.psum(grad_totals[0].astype(jnp.bfloat16), 'ctx').astype(jnp.float32)  350 us
    unnamed x31, waiting for transfers between devices  337 us
    all_gather x3, waiting for transfers between devices, layer_backward(): lax.all_gather(held_keys[1], 'ctx', axis=0, tiled=True)  81.1 us
    all_gather x3, waiting for transfers between devices, layer_backward(): lax.all_gather(held_keys[0], 'ctx', axis=0, tiled=True)  71 us
    psum x3, waiting for transfers between devices, layer_backward(): lax.psum(jnp.dot(d_pre_bf, w_fc.T, preferred_element_type=jnp.float32).as...  64 us
    all_to_all x3, waiting for transfers between devices, layer_forward(): lax.all_to_all(jnp.stack([key_rows] * lax.axis_size('ctx')), 'ctx', 0, 0)  56.2 us
    all_gather x3, waiting for transfers between devices, layer_forward(): lax.all_gather(val_rows, 'ctx', axis=0, tiled=True)  51.3 us
    psum x2, waiting for transfers between devices, layer_forward(): lax.psum(jnp.dot(attended, w_out, preferred_element_type=jnp.float32).ast...  44.2 us
  transfers between devices with their start and end apart: 32, of which 29 were waited for; matrix products, arithmetic and copies ran while one was open for 15% of the time, Pallas kernels for 0%

profile of v1, /device:TPU:0, one launch (start us, length us, event | category | flops | bytes accessed | tf_op | source)
XLA Modules:
  0.0 1573.4 jit_solution(1017605978704812551)
XLA Ops:
  11.2 4.7 copy.76
  21.2 7.3 all-to-all-start
  30.7 27.7 %all-to-all-done = bf16[8,128,512]{1,2,0:T(8,128)(2,1)S(1)} async-done(((bf16[8,128,512]{1,2,0:T(8,128)(2,1)}), bf16[8,128,512]{1,2,0:T(8,128)(2,1)S(1)}, u32[]{:S(2)}, u32[]{:S(2)}) %all-to-all-start) | async-done | bytes 1048608 | tf_op jit(solution)/shard_map/all_to_all | solution.py:90
  61.5 3.2 fusion.24
  64.7 13.4 all-gather.10.cloned.1.call-done
  83.9 22.0 %all-reduce.16.cloned.1.call-done = bf16[128,1024]{1,0:T(8,128)(2,1)} async-done(((bf16[128,1024]{1,0:T(8,128)(2,1)}), bf16[128,1024]{1,0:T(8,128)(2,1)}) %all-reduce.16.cloned.1.call-update) | async-done | bytes 262160 | tf_op jit(solution)/shard_map/psum | solution.py:105
  108.5 3.1 fusion.35
  113.4 23.4 %all-reduce.18.cloned.1.call-done = bf16[128,1024]{1,0:T(8,128)(2,1)} async-done(((bf16[128,1024]{1,0:T(8,128)(2,1)}), bf16[128,1024]{1,0:T(8,128)(2,1)}) %all-reduce.18.cloned.1.call-update) | async-done | bytes 262160 | tf_op jit(solution)/shard_map/psum | solution.py:116
  148.1 5.5 all-to-all-start.1
  155.7 28.5 %all-to-all-done.1 = bf16[8,128,512]{1,2,0:T(8,128)(2,1)} async-done(((bf16[8,128,512]{1,2,0:T(8,128)(2,1)}), bf16[8,128,512]{1,2,0:T(8,128)(2,1)}, u32[]{:S(2)}, u32[]{:S(2)}) %all-to-all-start.1) | async-done | bytes 1048608 | tf_op jit(solution)/shard_map/all_to_all | solution.py:90
  189.5 5.0 fusion.26
  194.5 9.0 all-gather.12.cloned.1.call-done
  205.7 3.4 fusion.132
  210.2 22.1 %all-reduce.20.cloned.1.call-done = bf16[128,1024]{1,0:T(8,128)(2,1)} async-done(((bf16[128,1024]{1,0:T(8,128)(2,1)}), bf16[128,1024]{1,0:T(8,128)(2,1)}) %all-reduce.20.cloned.1.call-update) | async-done | bytes 262160 | tf_op jit(solution)/shard_map/psum | solution.py:105
  235.5 3.1 fusion.38
  247.1 28.0 %all-reduce.34.cloned.1.call-done = (bf16[128,1024]{1,0:T(8,128)(2,1)}, bf16[128,1024]{1,0:T(8,128)(2,1)}) async-done(((bf16[128,1024]{1,0:T(8,128)(2,1)}, bf16[128,1024]{1,0:T(8,128)(2,1)}), (bf16[128,1024]{1,0:T(8,128)(2,1)}, bf16[128,1024]{1,0:T(8,128)(2,1)})) %all-reduce.34.cloned.1.call-update) | async-done | bytes 524304 | tf_op jit(solution)/shard_map/psum | solution.py:166
  287.1 5.5 all-to-all-start.2
  292.9 35.1 %all-gather.16.cloned.1.call-done = bf16[1024,512]{1,0:T(8,128)(2,1)} async-done(((bf16[128,512]{1,0:T(8,128)(2,1)}), bf16[1024,512]{1,0:T(8,128)(2,1)}) %all-gather.16.cloned.1.call-update) | async-done | bytes 1048592 | tf_op jit(solution)/shard_map/all_gather | solution.py:178
  330.3 4.0 fusion.384
  345.6 4.6 fusion.28
  355.4 13.7 all-gather.18.cloned.1.call-done
  372.1 4.1 multiply_convert_fusion.2
  381.3 28.9 %all-gather.14.cloned.1.call-done = bf16[1024,512]{1,0:T(8,128)(2,1)} async-done(((bf16[128,512]{1,0:T(8,128)(2,1)}), bf16[1024,512]{1,0:T(8,128)(2,1)}) %all-gather.14.cloned.1.call-update) | async-done | bytes 1048592 | tf_op jit(solution)/shard_map/all_gather | solution.py:92
  412.5 3.5 fusion.126
  418.6 58.5 %reduce-scatter.21.cloned.1.call-done = bf16[128,512]{1,0:T(8,128)(2,1)} async-done(((bf16[1024,512]{1,0:T(8,128)(2,1)}), bf16[128,512]{1,0:T(8,128)(2,1)}) %reduce-scatter.21.cloned.1.call-update) | async-done | bytes 131088
  478.1 65.7 %reduce-scatter.19.cloned.1.call-done = bf16[128,512]{1,0:T(8,128)(2,1)} async-done(((bf16[1024,512]{1,0:T(8,128)(2,1)}), bf16[128,512]{1,0:T(8,128)(2,1)}) %reduce-scatter.19.cloned.1.call-update) | async-done | bytes 131088
  544.9 3.3 convolution_convert_fusion.2
  549.9 26.0 %all-reduce.32.cloned.1.call-done = (bf16[128,1024]{1,0:T(8,128)(2,1)}, bf16[128,1024]{1,0:T(8,128)(2,1)}) async-done(((bf16[128,1024]{1,0:T(8,128)(2,1)}, bf16[128,1024]{1,0:T(8,128)(2,1)}), (bf16[128,1024]{1,0:T(8,128)(2,1)}, bf16[128,1024]{1,0:T(8,128)(2,1)})) %all-reduce.32.cloned.1.call-update) | async-done | bytes 524304 | tf_op jit(solution)/shard_map/psum | solution.py:226
  585.2 3.2 fusion.41
  595.9 23.0 %all-gather.20.cloned.1.call-done = bf16[1024,512]{1,0:T(8,128)(2,1)} async-done(((bf16[128,512]{1,0:T(8,128)(2,1)}), bf16[1024,512]{1,0:T(8,128)(2,1)}) %all-gather.20.cloned.1.call-update) | async-done | bytes 1048592 | tf_op jit(solution)/shard_map/all_gather | solution.py:178
  621.1 4.0 fusion.385
  625.1 18.5 %all-reduce.22.cloned.1.call-done = bf16[128,1024]{1,0:T(8,128)(2,1)} async-done(((bf16[128,1024]{1,0:T(8,128)(2,1)}), bf16[128,1024]{1,0:T(8,128)(2,1)}) %all-reduce.22.cloned.1.call-update) | async-done | bytes 262160 | tf_op jit(solution)/shard_map/psum | solution.py:166
  650.5 4.3 fusion.89
  657.1 28.7 %all-gather.22.cloned.1.call-done = bf16[1024,512]{1,0:T(8,128)(2,1)} async-done(((bf16[128,512]{1,0:T(8,128)(2,1)}), bf16[1024,512]{1,0:T(8,128)(2,1)}) %all-gather.22.cloned.1.call-update) | async-done | bytes 1048592 | tf_op jit(solution)/shard_map/all_gather | solution.py:179
  689.8 4.2 multiply_convert_fusion.1
  699.6 6.1 fusion.275
  705.7 4.9 fusion.245
  714.0 12.9 all-gather.24.cloned.1.call-done
  729.2 38.7 %all-gather.26.cloned.1.call-done = bf16[1024,512]{1,0:T(8,128)(2,1)} async-done(((bf16[128,512]{1,0:T(8,128)(2,1)}), bf16[1024,512]{1,0:T(8,128)(2,1)}) %all-gather.26.cloned.1.call-update) | async-done | bytes 1048592 | tf_op jit(solution)/shard_map/all_gather | solution.py:179
  770.2 4.3 fusion.386
  776.5 57.6 %reduce-scatter.25.cloned.1.call-done = bf16[128,512]{1,0:T(8,128)(2,1)} async-done(((bf16[1024,512]{1,0:T(8,128)(2,1)}), bf16[128,512]{1,0:T(8,128)(2,1)}) %reduce-scatter.25.cloned.1.call-update) | async-done | bytes 131088
  835.8 64.9 %reduce-scatter.23.cloned.1.call-done = bf16[128,512]{1,0:T(8,128)(2,1)} async-done(((bf16[1024,512]{1,0:T(8,128)(2,1)}), bf16[128,512]{1,0:T(8,128)(2,1)}) %reduce-scatter.23.cloned.1.call-update) | async-done | bytes 131088
  902.3 3.4 convolution_convert_fusion.1
  905.8 4.9 fusion.280
  910.7 17.4 %all-reduce.24.cloned.1.call-done = bf16[128,1024]{1,0:T(8,128)(2,1)} async-done(((bf16[128,1024]{1,0:T(8,128)(2,1)}), bf16[128,1024]{1,0:T(8,128)(2,1)}) %all-reduce.24.cloned.1.call-update) | async-done | bytes 262160 | tf_op jit(solution)/shard_map/psum | solution.py:226
  934.8 3.7 fusion.111
  944.9 6.6 fusion.243
  951.5 17.5 %all-reduce.26.cloned.1.call-done = bf16[128,1024]{1,0:T(8,128)(2,1)} async-done(((bf16[128,1024]{1,0:T(8,128)(2,1)}), bf16[128,1024]{1,0:T(8,128)(2,1)}) %all-reduce.26.cloned.1.call-update) | async-done | bytes 262160 | tf_op jit(solution)/shard_map/psum | solution.py:166
  976.4 4.3 fusion.92
  983.2 6.1 fusion.273
  991.1 3.9 fusion.278
  1002.5 9.6 fusion.30
  1012.2 9.2 fusion.31
  1025.2 22.3 %reduce-scatter.29.cloned.1.call-done = bf16[128,512]{1,0:T(8,128)(2,1)} async-done(((bf16[1024,512]{1,0:T(8,128)(2,1)}), bf16[128,512]{1,0:T(8,128)(2,1)}) %reduce-scatter.29.cloned.1.call-update) | async-done | bytes 131088
  1048.5 65.6 %reduce-scatter.27.cloned.1.call-done = bf16[128,512]{1,0:T(8,128)(2,1)} async-done(((bf16[1024,512]{1,0:T(8,128)(2,1)}), bf16[128,512]{1,0:T(8,128)(2,1)}) %reduce-scatter.27.cloned.1.call-update) | async-done | bytes 131088
  1115.2 3.2 convolution_convert_fusion
  1118.5 7.6 add_convert_fusion.2
  1126.1 4.6 copy.101
  1141.0 5.2 all-reduce.30.cloned.1.call-done
  1149.0 38.9 %all-reduce = (bf16[1,2,512]{2,1,0:T(2,128)(2,1)S(1)}, bf16[1,1024]{1,0:T(2,128)(2,1)S(1)}, bf16[1,2048]{1,0:T(2,128)(2,1)S(1)}, bf16[1,1024]{1,0:T(2,128)(2,1)S...) all-reduce(bf16[1,2,512]{2,1,0:T(2,128)(2,1)S(1)} %fusion.327, ...), channel_id=1, replica_groups=mesh['section'=2,'ctx'=8,'tp'=2] {'ctx'}, use_global_device_ids=true, to_apply=%region_55.56 | all-reduce | flops 9216 | bytes 36864 | tf_op jit(solution)/shard_map/psum | solution.py:319
  1196.9 350.4 %all-reduce.28.cloned.1.call-done = (bf16[1,1024,3,512]{1,3,2,0:T(8,128)(2,1)}, bf16[1,512,1024]{2,1,0:T(8,128)(2,1)}, bf16[1,1024,2048]{2,1,0:T(8,128)(2,1)}, bf16[1,2048,1024]{2,1,0:T(8,128)(2,1)}) async-done(((bf16[1,1024,3,512]{1,3,2,0:T(8,128)(2,1)}, bf16[1,512,1024]{2,1,0:T(8,128)(2,1)}, bf16[1,1024,2048]{2,1,0:T(8,128)(2,1)}, bf16[1,2048,1024]{2,1,0:T(8,128)(2,1)}), ...) | async-done | bytes 12582928 | tf_op jit(solution)/shard_map/psum | solution.py:318
  1550.1 5.4 copy.102
  1555.4 6.8 broadcast_in_dim.177
  1562.2 4.4 broadcast_in_dim.181
  (541 shorter events, 218.6 us)
Async XLA Ops:
  7.2 75.6 %copy-start = (bf16[1,512,1024]{2,1,0:T(8,128)(2,1)S(1)}, bf16[1,512,1024]{2,1,0:T(8,128)(2,1)}, u32[]{:S(2)}) copy-start(bf16[1,512,1024]{2,1,0:T(8,128)(2,1)} %param.16) | copy-start | bytes 3145732
  11.2 97.4 %copy-start.83 = (f32[1,1,1024]{2,1,0:T(1,128)}, f32[1,1,1024]{2,1,0:T(1,128)S(1)}, u32[]{:S(2)}) copy-start(f32[1,1,1024]{2,1,0:T(1,128)S(1)} %get-tuple-element.132) | copy-start | bytes 12292
  21.2 37.2 %all-to-all-start = ((bf16[8,128,512]{1,2,0:T(8,128)(2,1)}), bf16[8,128,512]{1,2,0:T(8,128)(2,1)S(1)}, u32[]{:S(2)}, u32[]{:S(2)}) async-start(bf16[8,128,512]{1,2,0:T(8,128)(2,1)} %stack.132), calls=%async_computation | async-start | bytes 2097152 | tf_op jit(solution)/shard_map/all_to_all | solution.py:90
  28.5 49.7 %all-gather.10.cloned.1.call-start = ((), (), s32[]{:S(2)}) async-start(), calls=%async_computation.9 | async-start | bytes 1179648 | tf_op jit(solution)/shard_map/all_gather | solution.py:92
  30.3 114.7 %copy-start.50 = (bf16[128,512]{1,0:T(8,128)(2,1)}, bf16[128,512]{1,0:T(8,128)(2,1)S(1)}, u32[]{:S(2)}) copy-start(bf16[128,512]{1,0:T(8,128)(2,1)S(1)} %get-tuple-element.120) | copy-start | bytes 393220
  30.3 75.7 %all-reduce.16.cloned.1.call-start = ((), (), s32[]{:S(2)}) async-start(), calls=%async_computation.10 | async-start | bytes 524288 | tf_op jit(solution)/shard_map/psum | solution.py:105
  30.7 49.0 %copy-start.92 = (pred[128,1024]{1,0:T(8,128)(4,1)}, pred[128,1024]{1,0:T(8,128)(4,1)S(1)}, u32[]{:S(2)}) copy-start(pred[128,1024]{1,0:T(8,128)(4,1)S(1)} %iota_compare_fusion) | copy-start | bytes 393220
  83.8 53.0 %all-reduce.18.cloned.1.call-start = ((), (), s32[]{:S(2)}) async-start(), calls=%async_computation.11 | async-start | bytes 524288 | tf_op jit(solution)/shard_map/psum | solution.py:116
  111.7 128.4 %copy-start.8 = (f32[128,2048]{1,0:T(8,128)}, f32[128,2048]{1,0:T(8,128)S(1)}, u32[]{:S(2)}) copy-start(f32[128,2048]{1,0:T(8,128)S(1)} %fusion.35) | copy-start | bytes 3145732
  138.0 2.4 collective-permute-start
  146.8 47.6 %copy-start.66 = (bf16[128,512]{1,0:T(8,128)(2,1)}, bf16[128,512]{1,0:T(8,128)(2,1)S(1)}, u32[]{:S(2)}) copy-start(bf16[128,512]{1,0:T(8,128)(2,1)S(1)} %get-tuple-element.105) | copy-start | bytes 393220
  146.8 42.6 %copy-start.93 = (pred[128,1024]{1,0:T(8,128)(4,1)S(1)}, pred[128,1024]{1,0:T(8,128)(4,1)}, u32[]{:S(2)}) copy-start(pred[128,1024]{1,0:T(8,128)(4,1)} %copy-done.92) | copy-start | bytes 393220
  148.1 36.2 %all-to-all-start.1 = ((bf16[8,128,512]{1,2,0:T(8,128)(2,1)}), bf16[8,128,512]{1,2,0:T(8,128)(2,1)}, u32[]{:S(2)}, u32[]{:S(2)}) async-start(bf16[8,128,512]{1,2,0:T(8,128)(2,1)} %stack.133), calls=%async_computation.1 | async-start | bytes 2097152 | tf_op jit(solution)/shard_map/all_to_all | solution.py:90
  153.6 49.9 %all-gather.12.cloned.1.call-start = ((), (), s32[]{:S(2)}) async-start(), calls=%async_computation.12 | async-start | bytes 1179648 | tf_op jit(solution)/shard_map/all_gather | solution.py:92
  154.2 78.2 %all-reduce.20.cloned.1.call-start = ((), (), s32[]{:S(2)}) async-start(), calls=%async_computation.13 | async-start | bytes 524288 | tf_op jit(solution)/shard_map/psum | solution.py:105
  209.1 162.2 %copy-start.58 = (bf16[128,8,64]{0,2,1:T(8,128)(2,1)}, bf16[128,8,64]{0,2,1:T(8,128)(2,1)S(1)}, u32[]{:S(2)}) copy-start(bf16[128,8,64]{0,2,1:T(8,128)(2,1)S(1)} %fusion.132) | copy-start | bytes 393220
  210.2 64.9 %all-reduce.34.cloned.1.call-start = ((), (), s32[]{:S(2)}) async-start(), calls=%async_computation.33 | async-start | bytes 1048576 | tf_op jit(solution)/shard_map/psum | solution.py:166
  246.3 81.7 %all-gather.16.cloned.1.call-start = ((), (), s32[]{:S(2)}) async-start(), calls=%async_computation.15 | async-start | bytes 1179648 | tf_op jit(solution)/shard_map/all_gather | solution.py:178
  247.0 122.0 %all-gather.18.cloned.1.call-start = ((), (), s32[]{:S(2)}) async-start(), calls=%async_computation.16 | async-start | bytes 1179648 | tf_op jit(solution)/shard_map/all_gather | solution.py:179
  277.0 2.7 collective-permute-start.1
  285.9 48.3 %copy-start.65 = (bf16[128,512]{1,0:T(8,128)(2,1)}, bf16[128,512]{1,0:T(8,128)(2,1)S(1)}, u32[]{:S(2)}) copy-start(bf16[128,512]{1,0:T(8,128)(2,1)S(1)} %get-tuple-element.91) | copy-start | bytes 393220
  285.9 53.7 %copy-start.64 = (bf16[128,512]{1,0:T(8,128)(2,1)}, bf16[128,512]{1,0:T(8,128)(2,1)S(1)}, u32[]{:S(2)}) copy-start(bf16[128,512]{1,0:T(8,128)(2,1)S(1)} %get-tuple-element.113) | copy-start | bytes 393220
  287.1 53.2 %all-to-all-start.2 = ((bf16[8,128,512]{1,2,0:T(8,128)(2,1)}), bf16[8,128,512]{1,2,0:T(8,128)(2,1)}, u32[]{:S(2)}, u32[]{:S(2)}) async-start(bf16[8,128,512]{1,2,0:T(8,128)(2,1)} %stack.135), calls=%async_computation.2 | async-start | bytes 2097152 | tf_op jit(solution)/shard_map/all_to_all | solution.py:90
  292.7 41.8 %copy-start.80 = (bf16[128,1024]{1,0:T(8,128)(2,1)S(1)}, bf16[128,1024]{1,0:T(8,128)(2,1)}, u32[]{:S(2)}) copy-start(bf16[128,1024]{1,0:T(8,128)(2,1)} %get-tuple-element.74) | copy-start | bytes 786436
  292.7 117.6 %all-gather.14.cloned.1.call-start = ((), (), s32[]{:S(2)}) async-start(), calls=%async_computation.14 | async-start | bytes 1179648 | tf_op jit(solution)/shard_map/all_gather | solution.py:92
  292.8 42.7 %copy-start.71 = (bf16[128,512]{0,1:T(8,128)(2,1)}, bf16[128,512]{0,1:T(8,128)(2,1)S(1)}, u32[]{:S(2)}) copy-start(bf16[128,512]{0,1:T(8,128)(2,1)S(1)} %copy.90) | copy-start | bytes 393220
  292.9 41.7 %copy-start.117 = (f32[128]{0:T(128)S(1)}, f32[128]{0:T(128)}, u32[]{:S(2)}) copy-start(f32[128]{0:T(128)} %copy-done.116) | copy-start | bytes 1540
  292.9 41.7 %copy-start.122 = (f32[128]{0:T(128)S(1)}, f32[128]{0:T(128)}, u32[]{:S(2)}) copy-start(f32[128]{0:T(128)} %copy-done.121) | copy-start | bytes 1540
  292.9 41.7 %copy-start.128 = (f32[128]{0:T(128)S(1)}, f32[128]{0:T(128)}, u32[]{:S(2)}) copy-start(f32[128]{0:T(128)} %copy-done.127) | copy-start | bytes 1540
  292.9 41.7 %copy-start.134 = (f32[128]{0:T(128)S(1)}, f32[128]{0:T(128)}, u32[]{:S(2)}) copy-start(f32[128]{0:T(128)} %copy-done.133) | copy-start | bytes 1540
  334.3 142.8 %reduce-scatter.21.cloned.1.call-start = ((), (), s32[]{:S(2)}) async-start(), calls=%async_computation.25 | async-start | bytes 1179648
  337.4 240.4 %copy-start.29 = (f32[128,1024]{1,0:T(8,128)}, f32[128,1024]{1,0:T(8,128)S(1)}, u32[]{:S(2)}) copy-start(f32[128,1024]{1,0:T(8,128)S(1)} %get-tuple-element.79) | copy-start | bytes 1572868
  355.4 188.5 %reduce-scatter.19.cloned.1.call-start = ((), (), s32[]{:S(2)}) async-start(), calls=%async_computation.24 | async-start | bytes 1179648
  381.3 194.6 %all-reduce.32.cloned.1.call-start = ((), (), s32[]{:S(2)}) async-start(), calls=%async_computation.32 | async-start | bytes 1048576 | tf_op jit(solution)/shard_map/psum | solution.py:226
  418.6 162.7 %copy-start.54 = (bf16[8,64,128]{2,1,0:T(8,128)(2,1)}, bf16[8,64,128]{2,1,0:T(8,128)(2,1)S(1)}, u32[]{:S(2)}) copy-start(bf16[8,64,128]{2,1,0:T(8,128)(2,1)S(1)} %get-tuple-element.124) | copy-start | bytes 393220
  548.1 70.7 %all-gather.20.cloned.1.call-start = ((), (), s32[]{:S(2)}) async-start(), calls=%async_computation.18 | async-start | bytes 1179648 | tf_op jit(solution)/shard_map/all_gather | solution.py:178
  549.8 93.8 %all-reduce.22.cloned.1.call-start = ((), (), s32[]{:S(2)}) async-start(), calls=%async_computation.17 | async-start | bytes 524288 | tf_op jit(solution)/shard_map/psum | solution.py:166
  581.3 7.2 collective-permute-start.2
  593.9 92.0 %all-gather.22.cloned.1.call-start = ((), (), s32[]{:S(2)}) async-start(), calls=%async_computation.19 | async-start | bytes 1179648 | tf_op jit(solution)/shard_map/all_gather | solution.py:179
  594.7 132.2 %all-gather.24.cloned.1.call-start = ((), (), s32[]{:S(2)}) async-start(), calls=%async_computation.22 | async-start | bytes 1179648 | tf_op jit(solution)/shard_map/all_gather | solution.py:178
  594.7 48.9 %copy-start.7 = (bf16[128,1024]{1,0:T(8,128)(2,1)S(1)}, bf16[128,1024]{1,0:T(8,128)(2,1)}, u32[]{:S(2)}) copy-start(bf16[128,1024]{1,0:T(8,128)(2,1)} %get-tuple-element.73) | copy-start | bytes 786436
  594.8 48.9 %copy-start.118 = (f32[128]{0:T(128)S(1)}, f32[128]{0:T(128)}, u32[]{:S(2)}) copy-start(f32[128]{0:T(128)} %copy-done.116) | copy-start | bytes 1540
  594.8 48.9 %copy-start.123 = (f32[128]{0:T(128)S(1)}, f32[128]{0:T(128)}, u32[]{:S(2)}) copy-start(f32[128]{0:T(128)} %copy-done.121) | copy-start | bytes 1540
  594.8 48.8 %copy-start.125 = (f32[128]{0:T(128)S(1)}, f32[128]{0:T(128)}, u32[]{:S(2)}) copy-start(f32[128]{0:T(128)} %copy-done.124) | copy-start | bytes 1540
  594.8 48.8 %copy-start.131 = (f32[128]{0:T(128)S(1)}, f32[128]{0:T(128)}, u32[]{:S(2)}) copy-start(f32[128]{0:T(128)} %copy-done.130) | copy-start | bytes 1540
  595.3 172.6 %all-gather.26.cloned.1.call-start = ((), (), s32[]{:S(2)}) async-start(), calls=%async_computation.23 | async-start | bytes 1179648 | tf_op jit(solution)/shard_map/all_gather | solution.py:179
  595.5 50.2 %copy-start.73 = (bf16[128,512]{0,1:T(8,128)(2,1)}, bf16[128,512]{0,1:T(8,128)(2,1)S(1)}, u32[]{:S(2)}) copy-start(bf16[128,512]{0,1:T(8,128)(2,1)S(1)} %copy.94) | copy-start | bytes 393220
  595.8 238.2 %reduce-scatter.25.cloned.1.call-start = ((), (), s32[]{:S(2)}) async-start(), calls=%async_computation.27 | async-start | bytes 1179648
  657.1 243.5 %reduce-scatter.23.cloned.1.call-start = ((), (), s32[]{:S(2)}) async-start(), calls=%async_computation.26 | async-start | bytes 1179648
  699.1 229.0 %all-reduce.24.cloned.1.call-start = ((), (), s32[]{:S(2)}) async-start(), calls=%async_computation.20 | async-start | bytes 524288 | tf_op jit(solution)/shard_map/psum | solution.py:226
  905.7 63.2 %all-reduce.26.cloned.1.call-start = ((), (), s32[]{:S(2)}) async-start(), calls=%async_computation.21 | async-start | bytes 524288 | tf_op jit(solution)/shard_map/psum | solution.py:166
  933.2 5.3 collective-permute-start.3
  944.7 102.8 %reduce-scatter.29.cloned.1.call-start = ((), (), s32[]{:S(2)}) async-start(), calls=%async_computation.29 | async-start | bytes 1179648
  983.1 131.1 %reduce-scatter.27.cloned.1.call-start = ((), (), s32[]{:S(2)}) async-start(), calls=%async_computation.28 | async-start | bytes 1179648
  1002.2 144.0 %all-reduce.30.cloned.1.call-start = ((), (), s32[]{:S(2)}) async-start(), calls=%async_computation.31 | async-start | bytes 1048576 | tf_op jit(solution)/shard_map/psum | solution.py:116
  1023.7 94.8 %copy-start.104 = (f32[128]{0:T(128)S(1)}, f32[128]{0:T(128)}, u32[]{:S(2)}) copy-start(f32[128]{0:T(128)} %copy-done.103) | copy-start | bytes 1540
  1023.7 94.8 %copy-start.108 = (f32[128]{0:T(128)S(1)}, f32[128]{0:T(128)}, u32[]{:S(2)}) copy-start(f32[128]{0:T(128)} %copy-done.106) | copy-start | bytes 1540
  1023.7 94.8 %copy-start.111 = (f32[128]{0:T(128)S(1)}, f32[128]{0:T(128)}, u32[]{:S(2)}) copy-start(f32[128]{0:T(128)} %copy-done.109) | copy-start | bytes 1540
  1023.7 94.8 %copy-start.115 = (f32[128]{0:T(128)S(1)}, f32[128]{0:T(128)}, u32[]{:S(2)}) copy-start(f32[128]{0:T(128)} %copy-done.114) | copy-start | bytes 1540
  1048.5 77.6 %copy-start.48 = (bf16[128,512]{0,1:T(8,128)(2,1)}, bf16[128,512]{0,1:T(8,128)(2,1)S(1)}, u32[]{:S(2)}) copy-start(bf16[128,512]{0,1:T(8,128)(2,1)S(1)} %copy.114) | copy-start | bytes 393220
  1118.4 428.9 %all-reduce.28.cloned.1.call-start = ((), (), s32[]{:S(2)}) async-start(), calls=%async_computation.30 | async-start | bytes 25165824 | tf_op jit(solution)/shard_map/psum | solution.py:318
  1130.7 60.7 %copy-start.100 = (f32[1,1024]{1,0:T(1,128)S(1)}, f32[1,1024]{1,0:T(1,128)}, u32[]{:S(2)}) copy-start(f32[1,1024]{1,0:T(1,128)} %copy-done.98) | copy-start | bytes 12292
  1131.8 62.7 %copy-start.34 = (f32[128,1024]{1,0:T(8,128)S(1)}, f32[128,1024]{1,0:T(8,128)}, u32[]{:S(2)}) copy-start(f32[128,1024]{1,0:T(8,128)} %copy-done.33) | copy-start | bytes 1572868
  1132.4 63.4 %copy-start.49 = (f32[1,128,1024]{2,1,0:T(8,128)S(1)}, f32[1,128,1024]{2,1,0:T(8,128)}, u32[]{:S(2)}) copy-start(f32[1,128,1024]{2,1,0:T(8,128)} %get-tuple-element.82) | copy-start | bytes 1572868
  (126 other events, 1249.7 us)
Sparse Core Ops, SparseCore 0:
  31.4 46.6 all-gather.9
  84.0 21.9 all-reduce.15
  113.5 23.2 all-reduce.17
  156.8 46.6 all-gather.11
  210.3 21.9 all-reduce.19
  246.4 28.6 all-reduce.33
  277.8 50.1 all-gather.15
  330.1 38.9 all-gather.17
  371.2 38.9 all-gather.13
  414.1 63.0 reduce-scatter.20
  480.5 63.2 reduce-scatter.18
  548.3 27.5 all-reduce.31
  578.6 40.2 all-gather.19
  621.6 21.9 all-reduce.21
  645.6 40.2 all-gather.21
  687.9 38.9 all-gather.23
  728.9 38.9 all-gather.25
  771.1 62.8 reduce-scatter.24
  837.5 63.0 reduce-scatter.22
  905.9 22.2 all-reduce.23
  944.8 24.0 all-reduce.25
  983.2 64.2 reduce-scatter.28
  1050.9 63.2 reduce-scatter.26
  1118.5 27.5 all-reduce.29
  1152.1 395.1 all-reduce.27
